TPU v7x, 128 devices: a whole 4x4x4 slice. The times are simulated.
128 devices in a mesh: row: 16 (over z, x), col: 8 (over y, core).
Axes of the slice: x: 4, y: 4, z: 4, core: 2. Of those that a mesh axis runs over, the one named last changes fastest.
Arguments:
- diag_block: float32 [512, 512], replicated, may hold values from 0 to 21.885, as said below
- panel: float32 [32768, 512], P('row'), may hold values from -6 to 6
- block_mask: int32 [128, 2], replicated, may hold values 0 or 1
- slab: float32 [32768, 8192], P('row', 'col'), may hold values from -6 to 6
Outputs:
- factor_rows: float32 [32768, 512], P('row')
- updated: float32 [32768, 8192], P('row', 'col')
- growth: float32 [], replicated
Inputs may be any that keep to these rules, and one draw needn't show every extreme that they name: `diag_block`: symmetric; each diagonal entry exceeds the sum of the magnitudes of the other entries of its row by 1 or more.
All inputs are finite; a program needn't handle non-finite values.
Results may differ from a plain program's by a relative error of at most 0.000064.
Values sent between devices are 32-bit elements; how exact they have to be, the bound alone decides.
A program may use at most 128 MiB of HBM per device.

v0:
```python
import jax
import jax.numpy as jnp
from jax import lax
from jax.experimental import pallas as pl
from jax.experimental.pallas import tpu as pltpu
from jax.sharding import PartitionSpec as P

B = 256
PW = 512
COARSE = 7
FINE = 3
MESH = pl.DeviceIdType.MESH
f32 = jnp.float32
bf16 = jnp.bfloat16


def nn(a, b):
    return lax.dot_general(a, b, (((1,), (0,)), ((), ())), preferred_element_type=f32)


def nt(a, b):
    return lax.dot_general(a, b, (((1,), (1,)), ((), ())), preferred_element_type=f32)


def split(a):
    high = a.astype(bf16)
    return high, (a - high.astype(f32)).astype(bf16)


def nt3(ah, al, bh, bl):
    return nt(ah, bh) + (nt(ah, bl) + nt(al, bh))


def nn3(ah, al, bh, bl):
    return nn(ah, bh) + (nn(ah, bl) + nn(al, bh))


def rows_at(start, size):
    return pl.ds(pl.multiple_of(start, 16), size)


def front_kernel(
    diag_ref, mask_ref, panel_ref, rows_ref, ch_ref, cl_ref,
    ah, al, w, wh, wl, mine, need,
    panel_sem, rows_sem, self_sem, out_sem, in_sem, ring_send, ring_recv,
):
    row, col = lax.axis_index("row"), lax.axis_index("col")
    z, x = row // 4, row % 4
    y, core = col // 2, col % 2
    right, left = z * 4 + (x + 1) % 4, z * 4 + (x + 3) % 4
    up, down = ((z + 1) % 4) * 4 + x, ((z + 3) % 4) * 4 + x
    half = need.shape[0] // 2
    piece = half // 16

    is_source = row < 4
    is_self = jnp.logical_and(row == 0, y == 0)
    source = (y, z * 2 + core)

    def spot(which, dz, dx):
        if which == 0:
            return (dz * 4 + dx) * piece
        return half + (dx * 4 + dz) * piece

    def scatter(which, dx):
        start = spot(which, y, dx)
        return (
            panel_ref.at[rows_at(core * 2 * half + start, piece)],
            need.at[rows_at(start, piece)],
            (y * 4 + dx, row * 2 + core),
        )

    barrier = pltpu.get_barrier_semaphore()

    def greet(device):
        pl.semaphore_signal(barrier, inc=1, device_id=device, device_id_type=MESH)

    for other in (right, left, up, down):
        greet((other, col))

    @pl.when(jnp.logical_not(is_self))
    def _():
        greet(source)

    @pl.when(is_source)
    def _():
        for dx in range(1, 4):
            greet((y * 4 + dx, row * 2 + core))

    @pl.when(jnp.logical_and(is_source, jnp.logical_not(is_self)))
    def _():
        greet((y * 4, row * 2 + core))

    others = 1 - is_self.astype(jnp.int32)
    pl.semaphore_wait(barrier, 4 + others + jnp.where(is_source, 3 + others, 0))

    def remote(which, dx):
        src, dst, device = scatter(which, dx)
        return pltpu.make_async_remote_copy(
            src_ref=src, dst_ref=dst, send_sem=out_sem.at[which * 4 + dx], recv_sem=in_sem.at[which],
            device_id=device, device_id_type=MESH,
        )

    def own(which):
        src, dst, _ = scatter(which, 0)
        return pltpu.make_async_copy(src, dst, self_sem.at[which])

    @pl.when(is_source)
    def _():
        for dx in range(1, 4):
            for which in range(2):
                remote(which, dx).start()

    @pl.when(jnp.logical_and(is_source, jnp.logical_not(is_self)))
    def _():
        for which in range(2):
            remote(which, 0).start()

    @pl.when(is_self)
    def _():
        for which in range(2):
            own(which).start()

    fetch = pltpu.make_async_copy(panel_ref, mine, panel_sem)
    fetch.start()

    def hop(index, start, size, device):
        part = need.at[rows_at(start, size)]
        return pltpu.make_async_remote_copy(
            src_ref=part, dst_ref=part, send_sem=ring_send.at[index], recv_sem=ring_recv.at[index],
            device_id=(device, col), device_id_type=MESH,
        )

    lx, rx, dz, uz = (x + 3) % 4, (x + 1) % 4, (z + 3) % 4, (z + 1) % 4

    def sends(step):
        wide = piece * 4
        if step == 0:
            return [
                hop(0, spot(0, z, x), piece, right), hop(1, spot(0, z, x), piece, left),
                hop(2, spot(1, z, x), piece, up), hop(3, spot(1, z, x), piece, down),
            ]
        if step == 1:
            part = piece // 2
            return [
                hop(4, spot(0, z, lx), part, right), hop(5, spot(0, z, rx) + part, part, left),
                hop(6, spot(1, dz, x), part, up), hop(7, spot(1, uz, x) + part, part, down),
            ]
        if step == 2:
            return [
                hop(8, z * wide, wide, up), hop(9, z * wide, wide, down),
                hop(10, half + x * wide, wide, right), hop(11, half + x * wide, wide, left),
            ]
        part = wide // 2
        return [
            hop(12, dz * wide, part, up), hop(13, uz * wide + part, part, down),
            hop(14, half + lx * wide, part, right), hop(15, half + rx * wide + part, part, left),
        ]

    def launch(step):
        for copy in sends(step):
            copy.start()

    def arrive(step):
        for copy in sends(step):
            copy.wait_recv()

    a = diag_ref[...]
    r_id = lax.broadcasted_iota(jnp.int32, (PW, PW), 0)
    c_id = lax.broadcasted_iota(jnp.int32, (PW, PW), 1)
    on_diag = jnp.where(r_id == c_id, a, 0.0)
    scale_rows = lax.rsqrt(jnp.sum(on_diag, axis=1, keepdims=True))
    scale_cols = lax.rsqrt(jnp.sum(on_diag, axis=0, keepdims=True))
    scaled = a * scale_rows * scale_cols
    ah[...], al[...] = split(scaled)
    w[...] = jnp.where(r_id == c_id, 1.5 - 0.5 * scaled, jnp.where(r_id > c_id, -scaled, 0.0))

    rb = lax.broadcasted_iota(jnp.int32, (B, B), 0)
    cb = lax.broadcasted_iota(jnp.int32, (B, B), 1)

    def correction(gram):
        return jnp.where(rb == cb, 0.5 - 0.5 * gram, jnp.where(rb > cb, -gram, 0.0)).astype(bf16)

    def apply(w0, w1, x00, x10, x11):
        p00, p10, p11 = correction(x00), (-x10).astype(bf16), correction(x11)
        w[:B, :B] += nn(p00, w0)
        w[B:, :B] += nn(p10, w0) + nn(p11, w1[:, :B])
        w[B:, B:] += nn(p11, w1[:, B:])

    def coarse(_, carry):
        w0, w1 = w[:B, :B].astype(bf16), w[B:, :].astype(bf16)
        y0 = nn(w0, ah[:B, :B]).astype(bf16)
        y1 = nn(w1, ah[...]).astype(bf16)
        apply(w0, w1, nt(y0, w0), nt(y1[:, :B], w0), nt(y1, w1))
        return carry

    def fine(_, carry):
        w0h, w0l = split(w[:B, :B])
        w1h, w1l = split(w[B:, :])
        y0h, y0l = split(nn3(w0h, w0l, ah[:B, :B], al[:B, :B]))
        y1h, y1l = split(nn3(w1h, w1l, ah[...], al[...]))
        apply(
            w0h, w1h, nt3(y0h, y0l, w0h, w0l), nt3(y1h[:, :B], y1l[:, :B], w0h, w0l), nt3(y1h, y1l, w1h, w1l)
        )
        return carry

    lax.fori_loop(0, COARSE, coarse, 0)

    @pl.when(jnp.logical_not(is_self))
    def _():
        for which in range(2):
            remote(which, 0).wait_recv()

    @pl.when(is_self)
    def _():
        for which in range(2):
            own(which).wait()

    launch(0)
    lax.fori_loop(0, FINE, fine, 0)
    arrive(0)
    launch(1)
    wh[...], wl[...] = split(w[...] * scale_cols)
    fetch.wait()

    def solve(tile, block):
        left_part = tile[:, :B] * mask_ref[block, 0].astype(f32)
        right_part = tile[:, B:] * mask_ref[block, 1].astype(f32)
        lh, ll = split(left_part)
        rh, rl = split(right_part)
        first = nt3(lh, ll, wh[:B, :B], wl[:B, :B])
        second = nt3(lh, ll, wh[B:, :B], wl[B:, :B]) + nt3(rh, rl, wh[B:, B:], wl[B:, B:])
        return first, second

    tiles = mine.shape[0] // B

    def rows_out(t):
        part = rows_at(t * B, B)
        return pltpu.make_async_copy(mine.at[part], rows_ref.at[part], rows_sem.at[t])

    def solve_mine(t, carry):
        part = rows_at(t * B, B)
        first, second = solve(mine[part, :], row * tiles + t)
        mine[part, :B] = first
        mine[part, B:] = second
        rows_out(t).start()
        return carry

    lax.fori_loop(0, 2, solve_mine, 0)
    arrive(1)
    launch(2)
    lax.fori_loop(2, tiles, solve_mine, 0)
    arrive(2)
    launch(3)
    arrive(3)

    needed = need.shape[0] // B

    def solve_need(t, carry):
        part = rows_at(t * B, B)
        first, second = solve(need[part, :], col * needed + t)
        ch_ref[part, :B], cl_ref[part, :B] = split(first)
        ch_ref[part, B:], cl_ref[part, B:] = split(second)
        return carry

    lax.fori_loop(0, needed, solve_need, 0)

    for step in range(4):
        for copy in sends(step):
            copy.wait_send()

    @pl.when(is_source)
    def _():
        for dx in range(1, 4):
            for which in range(2):
                remote(which, dx).wait_send()

    @pl.when(jnp.logical_and(is_source, jnp.logical_not(is_self)))
    def _():
        for which in range(2):
            remote(which, 0).wait_send()

    for t in range(tiles):
        rows_out(t).wait()


def update_kernel(rows_ref, ch_ref, cl_ref, slab_ref, rows_out, out_ref, max_ref):
    @pl.when(pl.program_id(0) == 0)
    def _():
        max_ref[...] = jnp.zeros_like(max_ref)

    rows = rows_ref[...]
    rows_out[...] = rows
    rh, rl = split(rows)
    step = 256
    for at in range(0, out_ref.shape[1], step):
        part = pl.ds(at, step)
        value = slab_ref[:, part] - nt3(rh, rl, ch_ref[part, :], cl_ref[part, :])
        out_ref[:, part] = value
        size = jnp.abs(value)
        size = jnp.max(size.reshape(-1, 8, step), axis=0)
        max_ref[...] = jnp.maximum(max_ref[...], jnp.maximum(size[:, :128], size[:, 128:]))


def growth_kernel(in_ref, out_ref, mid, cols_in, rows_in, col_send, col_recv, row_send, row_recv):
    row, col = lax.axis_index("row"), lax.axis_index("col")
    rows, cols = lax.axis_size("row"), lax.axis_size("col")
    barrier = pltpu.get_barrier_semaphore()
    for d in range(1, cols):
        pl.semaphore_signal(barrier, inc=1, device_id=(row, (col + d) % cols), device_id_type=MESH)
    for d in range(1, rows):
        pl.semaphore_signal(barrier, inc=1, device_id=((row + d) % rows, col), device_id_type=MESH)
    pl.semaphore_wait(barrier, rows + cols - 2)

    first = [
        pltpu.make_async_remote_copy(
            src_ref=in_ref, dst_ref=cols_in.at[d - 1], send_sem=col_send.at[d - 1], recv_sem=col_recv.at[d - 1],
            device_id=(row, (col + d) % cols), device_id_type=MESH,
        )
        for d in range(1, cols)
    ]
    for copy in first:
        copy.start()
    best = in_ref[...]
    for d in range(1, cols):
        first[d - 1].wait_recv()
        best = jnp.maximum(best, cols_in[d - 1])
    mid[...] = best
    second = [
        pltpu.make_async_remote_copy(
            src_ref=mid, dst_ref=rows_in.at[d - 1], send_sem=row_send.at[d - 1], recv_sem=row_recv.at[d - 1],
            device_id=((row + d) % rows, col), device_id_type=MESH,
        )
        for d in range(1, rows)
    ]
    for copy in second:
        copy.start()
    for d in range(1, rows):
        second[d - 1].wait_recv()
        best = jnp.maximum(best, rows_in[d - 1])
    out_ref[0, 0] = jnp.max(best)
    for copy in first + second:
        copy.wait_send()


def body(diag_block, panel, block_mask, slab):
    rows_dev, cols_dev = slab.shape
    tiles = rows_dev // B
    vmem = pl.BlockSpec(memory_space=pltpu.VMEM)
    smem = pl.BlockSpec(memory_space=pltpu.SMEM)
    hbm = pl.BlockSpec(memory_space=pl.ANY)
    dma = pltpu.SemaphoreType.DMA
    rows, ch, cl = pl.pallas_call(
        front_kernel,
        out_shape=(
            jax.ShapeDtypeStruct((rows_dev, PW), f32),
            jax.ShapeDtypeStruct((cols_dev, PW), bf16),
            jax.ShapeDtypeStruct((cols_dev, PW), bf16),
        ),
        in_specs=[vmem, smem, hbm],
        out_specs=(hbm, vmem, vmem),
        scratch_shapes=[
            pltpu.VMEM((PW, PW), bf16),
            pltpu.VMEM((PW, PW), bf16),
            pltpu.VMEM((PW, PW), f32),
            pltpu.VMEM((PW, PW), bf16),
            pltpu.VMEM((PW, PW), bf16),
            pltpu.VMEM((rows_dev, PW), f32),
            pltpu.VMEM((cols_dev, PW), f32),
            dma,
            dma((tiles,)),
            dma((2,)),
            dma((8,)),
            dma((2,)),
            dma((16,)),
            dma((16,)),
        ],
        compiler_params=pltpu.CompilerParams(
            collective_id=0, has_side_effects=True, vmem_limit_bytes=32 << 20
        ),
        name="front",
    )(diag_block, block_mask, panel)

    out_rows, updated, peak = pl.pallas_call(
        update_kernel,
        grid=(tiles,),
        out_shape=(
            jax.ShapeDtypeStruct((rows_dev, PW), f32),
            jax.ShapeDtypeStruct((rows_dev, cols_dev), f32),
            jax.ShapeDtypeStruct((8, 128), f32),
        ),
        in_specs=[
            pl.BlockSpec((B, PW), lambda i: (i, 0)),
            pl.BlockSpec((cols_dev, PW), lambda i: (0, 0)),
            pl.BlockSpec((cols_dev, PW), lambda i: (0, 0)),
            pl.BlockSpec((B, cols_dev), lambda i: (i, 0)),
        ],
        out_specs=(
            pl.BlockSpec((B, PW), lambda i: (i, 0)),
            pl.BlockSpec((B, cols_dev), lambda i: (i, 0)),
            pl.BlockSpec((8, 128), lambda i: (0, 0)),
        ),
        compiler_params=pltpu.CompilerParams(vmem_limit_bytes=32 << 20),
        name="update",
    )(rows, ch, cl, slab)

    n_rows, n_cols = lax.axis_size("row"), lax.axis_size("col")
    growth = pl.pallas_call(
        growth_kernel,
        out_shape=jax.ShapeDtypeStruct((1, 1), f32),
        in_specs=[vmem],
        out_specs=smem,
        scratch_shapes=[
            pltpu.VMEM((8, 128), f32),
            pltpu.VMEM((n_cols - 1, 8, 128), f32),
            pltpu.VMEM((n_rows - 1, 8, 128), f32),
            dma((n_cols - 1,)),
            dma((n_cols - 1,)),
            dma((n_rows - 1,)),
            dma((n_rows - 1,)),
        ],
        compiler_params=pltpu.CompilerParams(collective_id=1, has_side_effects=True),
        name="growth",
    )(peak)
    return (out_rows, updated, growth.reshape(()))


def solution(mesh):
    in_specs = (P(), P("row", None), P(), P("row", "col"))
    out_specs = (P("row", None), P("row", "col"), P())
    return jax.shard_map(body, mesh=mesh, in_specs=in_specs, out_specs=out_specs, check_vma=False)
```

profile of v0, /device:TPU:1, one launch (start us, length us, event | category | flops | bytes accessed | tf_op | source)
XLA Modules:
  0.0 77.2 jit_solution(12765439964233159121)
XLA Ops:
  0.6 0.8 %copy.7.mask_ref = s32[128,2]{1,0:T(8,128)S(1)} copy(s32[128,2]{0,1:T(2,128)} %param.6) | data formatting | bytes 2048 | tf_op args[2]
  1.4 0.0 copy-start.1
  1.4 2.2 %copy-done.1 = f32[2048,512]{1,0:T(8,128)S(1)} copy-done((f32[2048,512]{1,0:T(8,128)S(1)}, f32[2048,512]{1,0:T(8,128)}, u32[]{:S(2)}) %copy-start.1) | copy-done | bytes 4194328
  3.6 0.0 copy-start.2
  3.6 1.2 %copy-done.2 = f32[512,512]{1,0:T(8,128)S(1)} copy-done((f32[512,512]{1,0:T(8,128)S(1)}, f32[512,512]{1,0:T(8,128)}, u32[]{:S(2)}) %copy-start.2) | copy-done | bytes 1048600
  4.8 40.1 %front.1 = (f32[2048,512]{1,0:T(8,128)S(1)}, bf16[1024,512]{1,0:T(8,128)(2,1)S(1)}, bf16[1024,512]{1,0:T(8,128)(2,1)S(1)}) custom-call(f32[512,512]{1,0:T(8,128)S(1)} %copy-done.2, s32[128,2]{1,0:T(8,128)S(1)} %copy.7.mask_ref, f32[2048,512]{1,0:T(8,128)S(1)} %copy-done.1), custom_call_target="tpu_custom_call" | custom-call | tf_op jit(solution)/shard_map/front/pallas_call | solution.py:352
  44.9 0.0 copy-start
  44.9 3.4 %copy-done = f32[2048,1024]{1,0:T(8,128)S(1)} copy-done((f32[2048,1024]{1,0:T(8,128)S(1)}, f32[2048,1024]{1,0:T(8,128)}, u32[]{:S(2)}) %copy-start) | copy-done | bytes 8388632
  48.3 9.5 %update.1 = (f32[2048,512]{1,0:T(8,128)}, f32[2048,1024]{1,0:T(8,128)}, f32[8,128]{1,0:T(8,128)S(1)}) custom-call(f32[2048,512]{1,0:T(8,128)S(1)} %get-tuple-element.9.rows_ref, bf16[1024,512]{1,0:T(8,128)(2,1)S(1)} %get-tuple-element.10.ch_ref, bf16[1024,512]{1,0:T(8,128)(2,1)S(1)} %get-tuple-element.11.cl_ref, f32[2048,1024]{1,0:T(8,128)S(1)} %copy-done), custom_call_target="tpu_custom_call" | custom-call | tf_op jit(solution)/shard_map/update/pallas_call | solution.py:383
  57.8 0.0 copy-start.3
  57.8 0.6 copy-done.3
  58.4 17.0 %growth.1 = f32[1,1]{1,0:T(1,128)} custom-call(f32[8,128]{1,0:T(8,128)} %copy-done.3), custom_call_target="tpu_custom_call" | custom-call | tf_op jit(solution)/shard_map/growth/pallas_call | solution.py:407
Async XLA Ops:
  1.4 2.2 %copy-start.1 = (f32[2048,512]{1,0:T(8,128)S(1)}, f32[2048,512]{1,0:T(8,128)}, u32[]{:S(2)}) copy-start(f32[2048,512]{1,0:T(8,128)} %panel_ref.1) | copy-start | bytes 12582916
  3.6 1.2 %copy-start.2 = (f32[512,512]{1,0:T(8,128)S(1)}, f32[512,512]{1,0:T(8,128)}, u32[]{:S(2)}) copy-start(f32[512,512]{1,0:T(8,128)} %diag_ref.1) | copy-start | bytes 3145732
  44.9 3.4 %copy-start = (f32[2048,1024]{1,0:T(8,128)S(1)}, f32[2048,1024]{1,0:T(8,128)}, u32[]{:S(2)}) copy-start(f32[2048,1024]{1,0:T(8,128)} %slab_ref.1) | copy-start | bytes 25165828
  57.8 0.6 copy-start.3
where the time goes:
time: 77.5 us; the launch traced here: 77.2 us
  Pallas kernels  66.5 us (86%)
  local copies, waits for them, and re-layouts  8.16 us (11%)
  between operations  2.48 us (3%)
    pallas_call x1, Pallas kernels, body(): pl.pallas_call(front_kernel, out_shape=(jax.ShapeDtypeStruct((rows_dev, P...  40.1 us
    pallas_call x1, Pallas kernels, body(): pl.pallas_call(growth_kernel, out_shape=jax.ShapeDtypeStruct((1, 1), f32)...  17 us
    pallas_call x1, Pallas kernels, body(): pl.pallas_call(update_kernel, grid=(tiles,), out_shape=(jax.ShapeDtypeStr...  9.5 us
    unnamed x9, local copies, waits for them, and re-layouts  8.16 us

commit v1 on v0

v1 whole, which is shorter than its diff:
```python
import jax
import jax.numpy as jnp
from jax import lax
from jax.experimental import pallas as pl
from jax.experimental.pallas import tpu as pltpu
from jax.sharding import PartitionSpec as P

B = 256
PW = 512
COARSE = 7
FINE = 3
MESH = pl.DeviceIdType.MESH
f32 = jnp.float32
bf16 = jnp.bfloat16


def nn(a, b):
    return lax.dot_general(a, b, (((1,), (0,)), ((), ())), preferred_element_type=f32)


def nt(a, b):
    return lax.dot_general(a, b, (((1,), (1,)), ((), ())), preferred_element_type=f32)


def split(a):
    high = a.astype(bf16)
    return high, (a - high.astype(f32)).astype(bf16)


def nt3(ah, al, bh, bl):
    return nt(ah, bh) + (nt(ah, bl) + nt(al, bh))


def nn3(ah, al, bh, bl):
    return nn(ah, bh) + (nn(ah, bl) + nn(al, bh))


def rows_at(start, size):
    return pl.ds(pl.multiple_of(start, 16), size)


def front_kernel(
    diag_hbm, mask_hbm, panel_hbm, slab_hbm, mine, near, slab_out,
    diag, mask, ah, al, w, wh, wl, need,
    diag_sem, mask_sem, panel_sem, slab_sem, self_sem, out_sem, in_sem, line_send, line_recv, ring_send, ring_recv,
):
    row, col = lax.axis_index("row"), lax.axis_index("col")
    z, x = row // 4, row % 4
    y, core = col // 2, col % 2
    half = need.shape[0] // 2
    piece = half // 16
    wide = 4 * piece

    is_source = row < 4
    is_self = jnp.logical_and(row == 0, y == 0)
    source = (y, z * 2 + core)

    def along_x(step):
        return z * 4 + (x + step) % 4

    def along_z(step):
        return ((z + step) % 4) * 4 + x

    fetch_diag = pltpu.make_async_copy(diag_hbm, diag, diag_sem)
    fetch_mask = pltpu.make_async_copy(mask_hbm, mask, mask_sem)
    fetch_panel = pltpu.make_async_copy(panel_hbm, mine, panel_sem)
    fetch_slab = pltpu.make_async_copy(slab_hbm, slab_out, slab_sem)
    fetch_diag.start()
    fetch_mask.start()

    barrier = pltpu.get_barrier_semaphore()

    def greet(device):
        pl.semaphore_signal(barrier, inc=1, device_id=device, device_id_type=MESH)

    @pl.when(jnp.logical_not(is_self))
    def _():
        greet(source)

    @pl.when(is_source)
    def _():
        for dx in range(1, 4):
            greet((y * 4 + dx, row * 2 + core))

    @pl.when(jnp.logical_and(is_source, jnp.logical_not(is_self)))
    def _():
        greet((y * 4, row * 2 + core))

    for step in range(1, 4):
        greet((along_x(step), col))
        greet((along_z(step), col))

    others = 1 - is_self.astype(jnp.int32)
    pl.semaphore_wait(barrier, 6 + others + jnp.where(is_source, 3 + others, 0))

    def spot(which, dz, dx):
        if which == 0:
            return (dz * 4 + dx) * piece
        return half + (dx * 4 + dz) * piece

    def scatter(which, dx):
        start = spot(which, y, dx)
        return (
            panel_hbm.at[rows_at(core * 2 * half + start, piece)],
            need.at[rows_at(start, piece)],
            (y * 4 + dx, row * 2 + core),
        )

    def remote(which, dx):
        src, dst, device = scatter(which, dx)
        return pltpu.make_async_remote_copy(
            src_ref=src, dst_ref=dst, send_sem=out_sem.at[which * 4 + dx], recv_sem=in_sem.at[which],
            device_id=device, device_id_type=MESH,
        )

    def own(which):
        src, dst, _ = scatter(which, 0)
        return pltpu.make_async_copy(src, dst, self_sem.at[which])

    @pl.when(is_source)
    def _():
        for which in range(2):
            for dx in range(1, 4):
                remote(which, dx).start()

    @pl.when(jnp.logical_and(is_source, jnp.logical_not(is_self)))
    def _():
        for which in range(2):
            remote(which, 0).start()

    @pl.when(is_self)
    def _():
        for which in range(2):
            own(which).start()

    fetch_panel.start()

    def hop(sems, index, start, size, device):
        part = need.at[rows_at(start, size)]
        return pltpu.make_async_remote_copy(
            src_ref=part, dst_ref=part, send_sem=sems[0].at[index], recv_sem=sems[1].at[index],
            device_id=(device, col), device_id_type=MESH,
        )

    line, ring = (line_send, line_recv), (ring_send, ring_recv)

    def line_hops(which):
        along = (along_x, along_z)[which]
        return [
            hop(line, 3 * which + step - 1, spot(which, z, x), piece, along(step)) for step in (2, 1, 3)
        ]

    def ring_hop(which, sign, stage):
        at, along = ((z, along_z), (x, along_x))[which]
        owner = at if stage < 2 else (at + 4 - sign) % 4
        part = stage % 2 if sign == 1 else 1 - stage % 2
        index = which * 6 + (0 if sign == 1 else 3) + stage
        return hop(ring, index, half * which + owner * wide + part * (wide // 2), wide // 2, along(sign % 4))

    fetch_diag.wait()
    a = diag[...]
    r_id = lax.broadcasted_iota(jnp.int32, (PW, PW), 0)
    c_id = lax.broadcasted_iota(jnp.int32, (PW, PW), 1)
    on_diag = jnp.where(r_id == c_id, a, 0.0)
    scale_rows = lax.rsqrt(jnp.sum(on_diag, axis=1, keepdims=True))
    scale_cols = lax.rsqrt(jnp.sum(on_diag, axis=0, keepdims=True))
    scaled = a * scale_rows * scale_cols
    ah[...], al[...] = split(scaled)
    w[...] = jnp.where(r_id == c_id, 1.5 - 0.5 * scaled, jnp.where(r_id > c_id, -scaled, 0.0))

    rb = lax.broadcasted_iota(jnp.int32, (B, B), 0)
    cb = lax.broadcasted_iota(jnp.int32, (B, B), 1)

    def correction(gram):
        return jnp.where(rb == cb, 0.5 - 0.5 * gram, jnp.where(rb > cb, -gram, 0.0)).astype(bf16)

    def apply(w0, w1, x00, x10, x11):
        p00, p10, p11 = correction(x00), (-x10).astype(bf16), correction(x11)
        w[:B, :B] += nn(p00, w0)
        w[B:, :B] += nn(p10, w0) + nn(p11, w1[:, :B])
        w[B:, B:] += nn(p11, w1[:, B:])

    def coarse(_, carry):
        w0, w1 = w[:B, :B].astype(bf16), w[B:, :].astype(bf16)
        y0 = nn(w0, ah[:B, :B]).astype(bf16)
        y1 = nn(w1, ah[...]).astype(bf16)
        apply(w0, w1, nt(y0, w0), nt(y1[:, :B], w0), nt(y1, w1))
        return carry

    def fine(_, carry):
        w0h, w0l = split(w[:B, :B])
        w1h, w1l = split(w[B:, :])
        y0h, y0l = split(nn3(w0h, w0l, ah[:B, :B], al[:B, :B]))
        y1h, y1l = split(nn3(w1h, w1l, ah[...], al[...]))
        apply(
            w0h, w1h, nt3(y0h, y0l, w0h, w0l), nt3(y1h[:, :B], y1l[:, :B], w0h, w0l), nt3(y1h, y1l, w1h, w1l)
        )
        return carry

    lax.fori_loop(0, COARSE, coarse, 0)

    @pl.when(jnp.logical_not(is_self))
    def _():
        for which in range(2):
            remote(which, 0).wait_recv()

    @pl.when(is_self)
    def _():
        for which in range(2):
            own(which).wait()

    for which in range(2):
        for copy in line_hops(which):
            copy.start()
    fetch_slab.start()
    lax.fori_loop(0, FINE, fine, 0)
    for which in range(2):
        for copy in line_hops(which):
            copy.wait_recv()
    for stage in range(2):
        for which in range(2):
            for sign in (1, -1):
                ring_hop(which, sign, stage).start()

    wh[...], wl[...] = split(w[...] * scale_cols)
    fetch_panel.wait()
    fetch_mask.wait()

    def solve(tile, block):
        left_part = tile[:, :B] * mask[0, block].astype(f32)
        right_part = tile[:, B:] * mask[1, block].astype(f32)
        lh, ll = split(left_part)
        rh, rl = split(right_part)
        first = nt3(lh, ll, wh[:B, :B], wl[:B, :B])
        second = nt3(lh, ll, wh[B:, :B], wl[B:, :B]) + nt3(rh, rl, wh[B:, B:], wl[B:, B:])
        return first, second

    tiles = mine.shape[0] // B

    def solve_mine(t, carry):
        part = rows_at(t * B, B)
        first, second = solve(mine[part, :], row * tiles + t)
        mine[part, :B] = first
        mine[part, B:] = second
        return carry

    def solve_need(start):
        part = rows_at(start, wide)
        first, second = solve(need[part, :], col * (2 * half // B) + start // B)
        for at, value in ((0, first), (B, second)):
            high, low = split(value)
            near[part, at:at + B] = high
            near[part, PW + at:PW + at + B] = low
            near[part, 2 * PW + at:2 * PW + at + B] = high

    lax.fori_loop(0, tiles, solve_mine, 0)
    for which in range(2):
        for sign in (1, -1):
            ring_hop(which, sign, 0).wait_recv()
            ring_hop(which, sign, 2).start()

    def quarter(which, step):
        return half * which + (((z, x)[which] + step) % 4) * wide

    for which in range(2):
        solve_need(quarter(which, 0))
    for which in range(2):
        for sign in (1, -1):
            ring_hop(which, sign, 1).wait_recv()
    for which in range(2):
        for step in (1, 3):
            solve_need(quarter(which, step))
    for which in range(2):
        for sign in (1, -1):
            ring_hop(which, sign, 2).wait_recv()
    for which in range(2):
        solve_need(quarter(which, 2))

    for which in range(2):
        for copy in line_hops(which):
            copy.wait_send()
        for sign in (1, -1):
            for stage in range(3):
                ring_hop(which, sign, stage).wait_send()

    @pl.when(is_source)
    def _():
        for dx in range(1, 4):
            for which in range(2):
                remote(which, dx).wait_send()

    @pl.when(jnp.logical_and(is_source, jnp.logical_not(is_self)))
    def _():
        for which in range(2):
            remote(which, 0).wait_send()

    fetch_slab.wait()


def update_kernel(rows_ref, near_ref, slab_ref, rows_out, out_ref, max_ref, rows_sem):
    tile = pl.program_id(0)

    @pl.when(tile == 0)
    def _():
        max_ref[...] = jnp.zeros_like(max_ref)
        pltpu.make_async_copy(rows_ref, rows_out, rows_sem).start()

    height = out_ref.shape[0]
    part = rows_at(tile * height, height)
    rh, rl = split(rows_ref[part, :])
    rows = jnp.concatenate([rh, rh, rl], axis=1)
    step = 256
    for at in range(0, out_ref.shape[1], step):
        value = slab_ref[part, at:at + step] - nt(rows, near_ref[at:at + step, :])
        out_ref[:, at:at + step] = value
        size = jnp.max(jnp.abs(value).reshape(-1, 8, step), axis=0)
        max_ref[...] = jnp.maximum(max_ref[...], jnp.maximum(size[:, :128], size[:, 128:]))

    @pl.when(tile == pl.num_programs(0) - 1)
    def _():
        pltpu.make_async_copy(rows_ref, rows_out, rows_sem).wait()


def far_first(size):
    return sorted(range(1, size), key=lambda d: -min(d, size - d))


def growth_kernel(in_ref, out_ref, mid, cols_in, rows_in, col_send, col_recv, row_send, row_recv):
    row, col = lax.axis_index("row"), lax.axis_index("col")
    rows, cols = lax.axis_size("row"), lax.axis_size("col")
    barrier = pltpu.get_barrier_semaphore()
    for d in range(1, cols):
        pl.semaphore_signal(barrier, inc=1, device_id=(row, (col + d) % cols), device_id_type=MESH)
    for d in range(1, rows):
        pl.semaphore_signal(barrier, inc=1, device_id=((row + d) % rows, col), device_id_type=MESH)
    pl.semaphore_wait(barrier, rows + cols - 2)

    first = {
        d: pltpu.make_async_remote_copy(
            src_ref=in_ref, dst_ref=cols_in.at[d - 1], send_sem=col_send.at[d - 1], recv_sem=col_recv.at[d - 1],
            device_id=(row, (col + d) % cols), device_id_type=MESH,
        )
        for d in far_first(cols)
    }
    for copy in first.values():
        copy.start()
    best = in_ref[...]
    for d in range(1, cols):
        first[d].wait_recv()
        best = jnp.maximum(best, cols_in[d - 1])
    mid[...] = best
    second = {
        d: pltpu.make_async_remote_copy(
            src_ref=mid, dst_ref=rows_in.at[d - 1], send_sem=row_send.at[d - 1], recv_sem=row_recv.at[d - 1],
            device_id=((row + d) % rows, col), device_id_type=MESH,
        )
        for d in far_first(rows)
    }
    for copy in second.values():
        copy.start()
    for d in range(1, rows):
        second[d].wait_recv()
        best = jnp.maximum(best, rows_in[d - 1])
    out_ref[0, 0] = jnp.max(best)
    for copy in [*first.values(), *second.values()]:
        copy.wait_send()


def body(diag_block, panel, block_mask, slab):
    rows_dev, cols_dev = slab.shape
    tiles = rows_dev // B
    vmem = pl.BlockSpec(memory_space=pltpu.VMEM)
    smem = pl.BlockSpec(memory_space=pltpu.SMEM)
    hbm = pl.BlockSpec(memory_space=pltpu.HBM)
    dma = pltpu.SemaphoreType.DMA
    marks = block_mask.T
    rows, near, slab_near = pl.pallas_call(
        front_kernel,
        out_shape=(
            jax.ShapeDtypeStruct((rows_dev, PW), f32),
            jax.ShapeDtypeStruct((cols_dev, 3 * PW), bf16),
            jax.ShapeDtypeStruct((rows_dev, cols_dev), f32),
        ),
        in_specs=[hbm, hbm, hbm, hbm],
        out_specs=(vmem, vmem, vmem),
        scratch_shapes=[
            pltpu.VMEM((PW, PW), f32),
            pltpu.SMEM(marks.shape, jnp.int32),
            pltpu.VMEM((PW, PW), bf16),
            pltpu.VMEM((PW, PW), bf16),
            pltpu.VMEM((PW, PW), f32),
            pltpu.VMEM((PW, PW), bf16),
            pltpu.VMEM((PW, PW), bf16),
            pltpu.VMEM((cols_dev, PW), f32),
            dma,
            dma,
            dma,
            dma,
            dma((2,)),
            dma((8,)),
            dma((2,)),
            dma((6,)),
            dma((6,)),
            dma((12,)),
            dma((12,)),
        ],
        compiler_params=pltpu.CompilerParams(
            collective_id=0, has_side_effects=True, vmem_limit_bytes=28 << 20
        ),
        name="front",
    )(*(pltpu.with_memory_space_constraint(a, pltpu.HBM) for a in (diag_block, marks, panel, slab)))

    out_rows, updated, peak = pl.pallas_call(
        update_kernel,
        grid=(tiles,),
        out_shape=(
            jax.ShapeDtypeStruct((rows_dev, PW), f32),
            jax.ShapeDtypeStruct((rows_dev, cols_dev), f32),
            jax.ShapeDtypeStruct((8, 128), f32),
        ),
        in_specs=[vmem, vmem, vmem],
        out_specs=(
            hbm,
            pl.BlockSpec((B, cols_dev), lambda i: (i, 0)),
            pl.BlockSpec((8, 128), lambda i: (0, 0)),
        ),
        scratch_shapes=[dma],
        compiler_params=pltpu.CompilerParams(vmem_limit_bytes=12 << 20),
        name="update",
    )(rows, near, slab_near)

    n_rows, n_cols = lax.axis_size("row"), lax.axis_size("col")
    growth = pl.pallas_call(
        growth_kernel,
        out_shape=jax.ShapeDtypeStruct((1, 1), f32),
        in_specs=[vmem],
        out_specs=smem,
        scratch_shapes=[
            pltpu.VMEM((8, 128), f32),
            pltpu.VMEM((n_cols - 1, 8, 128), f32),
            pltpu.VMEM((n_rows - 1, 8, 128), f32),
            dma((n_cols - 1,)),
            dma((n_cols - 1,)),
            dma((n_rows - 1,)),
            dma((n_rows - 1,)),
        ],
        compiler_params=pltpu.CompilerParams(collective_id=1, has_side_effects=True, vmem_limit_bytes=1 << 20),
        name="growth",
    )(peak)
    return (out_rows, updated, growth.reshape(()))


def solution(mesh):
    in_specs = (P(), P("row", None), P(), P("row", "col"))
    out_specs = (P("row", None), P("row", "col"), P())
    return jax.shard_map(body, mesh=mesh, in_specs=in_specs, out_specs=out_specs, check_vma=False)
```

time: 77.5 us -> 59.7 us (0.77)
  Pallas kernels: 66.5 us -> 57.1 us
  local copies, waits for them, and re-layouts: 8.16 us -> 0 us
    unnamed x9 -> x0, local copies, waits for them, and re-layouts: 8.16 us -> none
    pallas_call x1, Pallas kernels: 40.1 us -> 33.9 us  [body(): pl.pallas_call(front_kernel, out_shape=(jax.ShapeDtypeStruct((rows_dev, P...]
    pallas_call x1, Pallas kernels: 17 us -> 13.6 us  [body(): pl.pallas_call(growth_kernel, out_shape=jax.ShapeDtypeStruct((1, 1), f32)...]
where the time goes in v1:
time: 59.7 us; the launch traced here: 59.5 us
  Pallas kernels  57.1 us (96%)
  between operations  2.41 us (4%)
    pallas_call x1, Pallas kernels, body(): pl.pallas_call(front_kernel, out_shape=(jax.ShapeDtypeStruct((rows_dev, P...  33.9 us
    pallas_call x1, Pallas kernels, body(): pl.pallas_call(growth_kernel, out_shape=jax.ShapeDtypeStruct((1, 1), f32)...  13.6 us
    pallas_call x1, Pallas kernels, body(): pl.pallas_call(update_kernel, grid=(tiles,), out_shape=(jax.ShapeDtypeStr...  9.57 us

profile of v1, /device:TPU:1, one launch (start us, length us, event | category | flops | bytes accessed | tf_op | source)
XLA Modules:
  0.0 59.5 jit_solution(13846055433824596890)
XLA Ops:
  0.6 33.9 %front.1 = (f32[2048,512]{1,0:T(8,128)S(1)}, bf16[1024,1536]{1,0:T(8,128)(2,1)S(1)}, f32[2048,1024]{1,0:T(8,128)S(1)}) custom-call(f32[512,512]{1,0:T(8,128)} %diag_hbm.1, s32[2,128]{1,0:T(2,128)} %bitcast.2, f32[2048,512]{1,0:T(8,128)} %panel_hbm.1, f32[2048,1024]{1,0:T(8,128)} %slab_hbm.1), custom_call_target="tpu_custom_call" | custom-call | tf_op jit(solution)/shard_map/front/pallas_call | solution.py:377
  34.6 9.6 %update.1 = (f32[2048,512]{1,0:T(8,128)}, f32[2048,1024]{1,0:T(8,128)}, f32[8,128]{1,0:T(8,128)S(1)}) custom-call(f32[2048,512]{1,0:T(8,128)S(1)} %get-tuple-element.9.rows_ref, bf16[1024,1536]{1,0:T(8,128)(2,1)S(1)} %get-tuple-element.10.near_ref, f32[2048,1024]{1,0:T(8,128)S(1)} %get-tuple-element.11.slab_ref), custom_call_target="tpu_custom_call" | custom-call | tf_op jit(solution)/shard_map/update/pallas_call | solution.py:413
  44.2 13.6 %growth.1 = f32[1,1]{1,0:T(1,128)} custom-call(f32[8,128]{1,0:T(8,128)S(1)} %get-tuple-element.14.in_ref), custom_call_target="tpu_custom_call" | custom-call | tf_op jit(solution)/shard_map/growth/pallas_call | solution.py:433

commit v2 on v1

v2 whole, which is shorter than its diff:
```python
import jax
import jax.numpy as jnp
from jax import lax
from jax.experimental import pallas as pl
from jax.experimental.pallas import tpu as pltpu
from jax.sharding import PartitionSpec as P

B = 256
PW = 512
COARSE = 7
FINE = 2
EARLY = 3
TALL = 512
MESH = pl.DeviceIdType.MESH
f32 = jnp.float32
bf16 = jnp.bfloat16


def nn(a, b):
    return lax.dot_general(a, b, (((1,), (0,)), ((), ())), preferred_element_type=f32)


def nt(a, b):
    return lax.dot_general(a, b, (((1,), (1,)), ((), ())), preferred_element_type=f32)


def split(a):
    high = a.astype(bf16)
    return high, (a - high.astype(f32)).astype(bf16)


def nt3(ah, al, bh, bl):
    return nt(ah, bh) + (nt(ah, bl) + nt(al, bh))


def nn3(ah, al, bh, bl):
    return nn(ah, bh) + (nn(ah, bl) + nn(al, bh))


def rows_at(start, size):
    return pl.ds(pl.multiple_of(start, 16), size)


def far_first(size):
    return sorted(range(1, size), key=lambda d: -min(d, size - d))


def front_kernel(
    diag_hbm, mask_hbm, panel_hbm, slab_hbm, mine, slab, growth_ref,
    diag, mask, ah, al, w, wh, wl, rh, rl, gh, gl, need, peak, cols_in, rows_in,
    diag_sem, mask_sem, panel_sem, slab_sem, self_sem, out_sem, in_sem, line_send, line_recv, ring_send, ring_recv,
    col_send, col_recv, row_send, row_recv,
):
    row, col = lax.axis_index("row"), lax.axis_index("col")
    z, x = row // 4, row % 4
    y, core = col // 2, col % 2
    half = need.shape[0] // 2
    piece = half // 16
    wide = 4 * piece
    rows, cols = lax.axis_size("row"), lax.axis_size("col")

    is_source = row < 4
    is_self = jnp.logical_and(row == 0, y == 0)
    source = (y, z * 2 + core)

    def along_x(step):
        return z * 4 + (x + step) % 4

    def along_z(step):
        return ((z + step) % 4) * 4 + x

    fetch_diag = pltpu.make_async_copy(diag_hbm, diag, diag_sem)
    fetch_mask = pltpu.make_async_copy(mask_hbm, mask, mask_sem)
    fetch_panel = pltpu.make_async_copy(panel_hbm, mine, panel_sem)
    fetch_slab = pltpu.make_async_copy(slab_hbm, slab, slab_sem)
    fetch_diag.start()
    fetch_mask.start()

    barrier = pltpu.get_barrier_semaphore()

    def greet(device):
        pl.semaphore_signal(barrier, inc=1, device_id=device, device_id_type=MESH)

    @pl.when(jnp.logical_not(is_self))
    def _():
        greet(source)

    @pl.when(is_source)
    def _():
        for dx in range(1, 4):
            greet((y * 4 + dx, row * 2 + core))

    @pl.when(jnp.logical_and(is_source, jnp.logical_not(is_self)))
    def _():
        greet((y * 4, row * 2 + core))

    for step in range(1, 4):
        greet((along_x(step), col))
        greet((along_z(step), col))
    for d in range(1, cols):
        greet((row, (col + d) % cols))

    others = 1 - is_self.astype(jnp.int32)
    pl.semaphore_wait(barrier, 5 + cols + others + jnp.where(is_source, 3 + others, 0))

    def spot(which, dz, dx):
        if which == 0:
            return (dz * 4 + dx) * piece
        return half + (dx * 4 + dz) * piece

    def scatter(which, dx):
        start = spot(which, y, dx)
        return (
            panel_hbm.at[rows_at(core * 2 * half + start, piece)],
            need.at[rows_at(start, piece)],
            (y * 4 + dx, row * 2 + core),
        )

    def remote(which, dx):
        src, dst, device = scatter(which, dx)
        return pltpu.make_async_remote_copy(
            src_ref=src, dst_ref=dst, send_sem=out_sem.at[which * 4 + dx], recv_sem=in_sem.at[which],
            device_id=device, device_id_type=MESH,
        )

    def own(which):
        src, dst, _ = scatter(which, 0)
        return pltpu.make_async_copy(src, dst, self_sem.at[which])

    @pl.when(is_source)
    def _():
        for which in range(2):
            for dx in range(1, 4):
                remote(which, dx).start()

    @pl.when(jnp.logical_and(is_source, jnp.logical_not(is_self)))
    def _():
        for which in range(2):
            remote(which, 0).start()

    @pl.when(is_self)
    def _():
        for which in range(2):
            own(which).start()

    fetch_panel.start()

    def hop(sems, index, start, size, device):
        part = need.at[rows_at(start, size)]
        return pltpu.make_async_remote_copy(
            src_ref=part, dst_ref=part, send_sem=sems[0].at[index], recv_sem=sems[1].at[index],
            device_id=(device, col), device_id_type=MESH,
        )

    line, ring = (line_send, line_recv), (ring_send, ring_recv)

    def line_hops(which):
        along = (along_x, along_z)[which]
        return [
            hop(line, 3 * which + step - 1, spot(which, z, x), piece, along(step)) for step in (2, 1, 3)
        ]

    def ring_hop(which, sign, stage):
        at, along = ((z, along_z), (x, along_x))[which]
        owner = at if stage < 2 else (at + 4 - sign) % 4
        part = stage % 2 if sign == 1 else 1 - stage % 2
        index = which * 6 + (0 if sign == 1 else 3) + stage
        return hop(ring, index, half * which + owner * wide + part * (wide // 2), wide // 2, along(sign % 4))

    fetch_diag.wait()
    a = diag[...]
    r_id = lax.broadcasted_iota(jnp.int32, (PW, PW), 0)
    c_id = lax.broadcasted_iota(jnp.int32, (PW, PW), 1)
    on_diag = jnp.where(r_id == c_id, a, 0.0)
    scale_rows = lax.rsqrt(jnp.sum(on_diag, axis=1, keepdims=True))
    scale_cols = lax.rsqrt(jnp.sum(on_diag, axis=0, keepdims=True))
    scaled = a * scale_rows * scale_cols
    ah[...], al[...] = split(scaled)
    w[...] = jnp.where(r_id == c_id, 1.5 - 0.5 * scaled, jnp.where(r_id > c_id, -scaled, 0.0))

    rb = lax.broadcasted_iota(jnp.int32, (B, B), 0)
    cb = lax.broadcasted_iota(jnp.int32, (B, B), 1)

    def correction(gram):
        return jnp.where(rb == cb, 0.5 - 0.5 * gram, jnp.where(rb > cb, -gram, 0.0)).astype(bf16)

    def apply(w0, w1, x00, x10, x11):
        p00, p10, p11 = correction(x00), (-x10).astype(bf16), correction(x11)
        w[:B, :B] += nn(p00, w0)
        w[B:, :B] += nn(p10, w0) + nn(p11, w1[:, :B])
        w[B:, B:] += nn(p11, w1[:, B:])

    def coarse(_, carry):
        w0, w1 = w[:B, :B].astype(bf16), w[B:, :].astype(bf16)
        y0 = nn(w0, ah[:B, :B]).astype(bf16)
        y1 = nn(w1, ah[...]).astype(bf16)
        apply(w0, w1, nt(y0, w0), nt(y1[:, :B], w0), nt(y1, w1))
        return carry

    def fine(_, carry):
        w0h, w0l = split(w[:B, :B])
        w1h, w1l = split(w[B:, :])
        y0h, y0l = split(nn3(w0h, w0l, ah[:B, :B], al[:B, :B]))
        y1h, y1l = split(nn3(w1h, w1l, ah[...], al[...]))
        apply(
            w0h, w1h, nt3(y0h, y0l, w0h, w0l), nt3(y1h[:, :B], y1l[:, :B], w0h, w0l), nt3(y1h, y1l, w1h, w1l)
        )
        return carry

    lax.fori_loop(0, COARSE, coarse, 0)

    @pl.when(jnp.logical_not(is_self))
    def _():
        for which in range(2):
            remote(which, 0).wait_recv()

    @pl.when(is_self)
    def _():
        for which in range(2):
            own(which).wait()

    for which in range(2):
        for copy in line_hops(which):
            copy.start()
    fetch_slab.start()
    lax.fori_loop(0, FINE, fine, 0)
    wh[...], wl[...] = split(w[...] * scale_cols)
    fetch_panel.wait()
    fetch_mask.wait()

    def solve(left_part, right_part):
        lh, ll = split(left_part)
        qh, ql = split(right_part)
        first = nt3(lh, ll, wh[:B, :B], wl[:B, :B])
        second = nt3(lh, ll, wh[B:, :B], wl[B:, :B]) + nt3(qh, ql, wh[B:, B:], wl[B:, B:])
        return first, second

    tiles = mine.shape[0] // B

    def solve_mine(t, carry):
        part = rows_at(t * B, B)
        block = row * tiles + t
        parts = solve(mine[part, :B] * mask[0, block].astype(f32), mine[part, B:] * mask[1, block].astype(f32))
        for at, value in zip((0, B), parts):
            mine[part, at:at + B] = value
            rh[part, at:at + B], rl[part, at:at + B] = split(value)
        return carry

    lax.fori_loop(0, EARLY, solve_mine, 0)
    for which in range(2):
        for copy in line_hops(which):
            copy.wait_recv()
    for stage in range(2):
        for which in range(2):
            for sign in (1, -1):
                ring_hop(which, sign, stage).start()
    lax.fori_loop(EARLY, tiles, solve_mine, 0)
    for which in range(2):
        for sign in (1, -1):
            ring_hop(which, sign, 0).wait_recv()
            ring_hop(which, sign, 2).start()

    def masked_need(which, step):
        start = half * which + (((z, x)[which] + step) % 4) * wide
        part = rows_at(start, wide)
        block = col * (2 * half // B) + start // B
        left_part = need[part, :B] * mask[0, block].astype(f32)
        right_part = need[part, B:] * mask[1, block].astype(f32)
        return pl.ds(pl.multiple_of(start, 128), wide), left_part, right_part

    peak[...] = jnp.zeros_like(peak)

    def update(step):
        at0, left0, right0 = masked_need(0, step)
        at1, left1, right1 = masked_need(1, step)
        first, second = solve(jnp.concatenate([left0, left1], axis=0), jnp.concatenate([right0, right1], axis=0))
        gh[:, :B], gl[:, :B] = split(first)
        gh[:, B:], gl[:, B:] = split(second)

        def update_rows(t, carry):
            part = rows_at(t * TALL, TALL)
            product = nt3(rh[part, :], rl[part, :], gh[...], gl[...])
            for at, value in ((at0, product[:, :wide]), (at1, product[:, wide:])):
                value = slab[part, at] - value
                slab[part, at] = value
                size = jnp.max(jnp.abs(value).reshape(-1, 8, wide), axis=0)
                peak[0] = jnp.maximum(peak[0], size)
            return carry

        lax.fori_loop(0, mine.shape[0] // TALL, update_rows, 0)

    fetch_slab.wait()
    update(0)
    for which in range(2):
        for sign in (1, -1):
            ring_hop(which, sign, 1).wait_recv()
    update(1)
    update(3)
    for which in range(2):
        for sign in (1, -1):
            ring_hop(which, sign, 2).wait_recv()
    update(2)

    def share(src, dst, sems, d, device):
        return pltpu.make_async_remote_copy(
            src_ref=src, dst_ref=dst.at[d - 1], send_sem=sems[0].at[d - 1], recv_sem=sems[1].at[d - 1],
            device_id=device, device_id_type=MESH,
        )

    def share_cols(d):
        return share(peak.at[0], cols_in, (col_send, col_recv), d, (row, (col + d) % cols))

    def share_rows(d):
        return share(peak.at[1], rows_in, (row_send, row_recv), d, ((row + d) % rows, col))

    for d in far_first(cols):
        share_cols(d).start()
    best = peak[0]
    for d in range(1, cols):
        share_cols(d).wait_recv()
    for d in range(1, cols):
        best = jnp.maximum(best, cols_in[d - 1])
    peak[1] = best
    for d in far_first(rows):
        share_rows(d).start()

    for which in range(2):
        for copy in line_hops(which):
            copy.wait_send()
        for sign in (1, -1):
            for stage in range(3):
                ring_hop(which, sign, stage).wait_send()

    @pl.when(is_source)
    def _():
        for dx in range(1, 4):
            for which in range(2):
                remote(which, dx).wait_send()

    @pl.when(jnp.logical_and(is_source, jnp.logical_not(is_self)))
    def _():
        for which in range(2):
            remote(which, 0).wait_send()

    for d in range(1, cols):
        share_cols(d).wait_send()
    for d in range(1, rows):
        share_rows(d).wait_recv()
    for d in range(1, rows):
        best = jnp.maximum(best, rows_in[d - 1])
    growth_ref[0, 0] = jnp.max(best)
    for d in range(1, rows):
        share_rows(d).wait_send()


def store_kernel(rows_ref, slab_ref, rows_out, slab_out, sems):
    copies = []
    for src, dst in ((slab_ref, slab_out), (rows_ref, rows_out)):
        for at in range(0, src.shape[0], TALL):
            part = pl.ds(at, TALL)
            copies.append(pltpu.make_async_copy(src.at[part], dst.at[part], sems.at[len(copies)]))
    for copy in copies:
        copy.start()
    for copy in copies:
        copy.wait()


def body(diag_block, panel, block_mask, slab):
    rows_dev, cols_dev = slab.shape
    n_rows, n_cols = lax.axis_size("row"), lax.axis_size("col")
    vmem = pl.BlockSpec(memory_space=pltpu.VMEM)
    smem = pl.BlockSpec(memory_space=pltpu.SMEM)
    hbm = pl.BlockSpec(memory_space=pltpu.HBM)
    dma = pltpu.SemaphoreType.DMA
    marks = block_mask.T
    rows, updated, growth = pl.pallas_call(
        front_kernel,
        out_shape=(
            jax.ShapeDtypeStruct((rows_dev, PW), f32),
            jax.ShapeDtypeStruct((rows_dev, cols_dev), f32),
            jax.ShapeDtypeStruct((1, 1), f32),
        ),
        in_specs=[hbm, hbm, hbm, hbm],
        out_specs=(vmem, vmem, smem),
        scratch_shapes=[
            pltpu.VMEM((PW, PW), f32),
            pltpu.SMEM(marks.shape, jnp.int32),
            pltpu.VMEM((PW, PW), bf16),
            pltpu.VMEM((PW, PW), bf16),
            pltpu.VMEM((PW, PW), f32),
            pltpu.VMEM((PW, PW), bf16),
            pltpu.VMEM((PW, PW), bf16),
            pltpu.VMEM((rows_dev, PW), bf16),
            pltpu.VMEM((rows_dev, PW), bf16),
            pltpu.VMEM((B, PW), bf16),
            pltpu.VMEM((B, PW), bf16),
            pltpu.VMEM((cols_dev, PW), f32),
            pltpu.VMEM((2, 8, 128), f32),
            pltpu.VMEM((n_cols - 1, 8, 128), f32),
            pltpu.VMEM((n_rows - 1, 8, 128), f32),
            dma,
            dma,
            dma,
            dma,
            dma((2,)),
            dma((8,)),
            dma((2,)),
            dma((6,)),
            dma((6,)),
            dma((12,)),
            dma((12,)),
            dma((n_cols - 1,)),
            dma((n_cols - 1,)),
            dma((n_rows - 1,)),
            dma((n_rows - 1,)),
        ],
        compiler_params=pltpu.CompilerParams(
            collective_id=0, has_side_effects=True, vmem_limit_bytes=32 << 20
        ),
        name="front",
    )(*(pltpu.with_memory_space_constraint(a, pltpu.HBM) for a in (diag_block, marks, panel, slab)))

    out_rows, out_slab = pl.pallas_call(
        store_kernel,
        out_shape=(
            jax.ShapeDtypeStruct((rows_dev, PW), f32),
            jax.ShapeDtypeStruct((rows_dev, cols_dev), f32),
        ),
        in_specs=[vmem, vmem],
        out_specs=(hbm, hbm),
        scratch_shapes=[dma((2 * rows_dev // TALL,))],
        compiler_params=pltpu.CompilerParams(vmem_limit_bytes=1 << 20),
        name="store",
    )(rows, updated)
    return (out_rows, out_slab, growth.reshape(()))


def solution(mesh):
    in_specs = (P(), P("row", None), P(), P("row", "col"))
    out_specs = (P("row", None), P("row", "col"), P())
    return jax.shard_map(body, mesh=mesh, in_specs=in_specs, out_specs=out_specs, check_vma=False)
```

time: 59.7 us -> 59.8 us (level)
    pallas_call x1, Pallas kernels: 33.9 us -> 52.7 us  [body(): pl.pallas_call(front_kernel, out_shape=(jax.ShapeDtypeStruct((rows_dev, P...]
    pallas_call x2 -> x1, Pallas kernels: 23.2 us -> 4.63 us  [body(): pl.pallas_call(store_kernel, out_shape=(jax.ShapeDtypeStruct((rows_dev, P...]
where the time goes in v2:
time: 59.8 us; the launch traced here: 59.7 us
  Pallas kernels  57.3 us (96%)
  between operations  2.4 us (4%)
    pallas_call x1, Pallas kernels, body(): pl.pallas_call(front_kernel, out_shape=(jax.ShapeDtypeStruct((rows_dev, P...  52.7 us
    pallas_call x1, Pallas kernels, body(): pl.pallas_call(store_kernel, out_shape=(jax.ShapeDtypeStruct((rows_dev, P...  4.63 us

profile of v2, /device:TPU:1, one launch (start us, length us, event | category | flops | bytes accessed | tf_op | source)
XLA Modules:
  0.0 59.7 jit_solution(657744560823126483)
XLA Ops:
  0.6 52.7 %front.1 = (f32[2048,512]{1,0:T(8,128)S(1)}, f32[2048,1024]{1,0:T(8,128)S(1)}, f32[1,1]{1,0:T(1,128)}) custom-call(f32[512,512]{1,0:T(8,128)} %diag_hbm.1, s32[2,128]{1,0:T(2,128)} %bitcast.2, f32[2048,512]{1,0:T(8,128)} %panel_hbm.1, f32[2048,1024]{1,0:T(8,128)} %slab_hbm.1), custom_call_target="tpu_custom_call" | custom-call | tf_op jit(solution)/shard_map/front/pallas_call | solution.py:376
  53.3 4.6 %store.1 = (f32[2048,512]{1,0:T(8,128)}, f32[2048,1024]{1,0:T(8,128)}) custom-call(f32[2048,512]{1,0:T(8,128)S(1)} %get-tuple-element.8.rows_ref, f32[2048,1024]{1,0:T(8,128)S(1)} %get-tuple-element.9.slab_ref), custom_call_target="tpu_custom_call" | custom-call | tf_op jit(solution)/shard_map/store/pallas_call | solution.py:423

commit v3 on v2

--- a/solution.py
+++ b/solution.py
@@ -9,8 +9,10 @@
 PW = 512
 COARSE = 7
 FINE = 2
-EARLY = 3
+EARLY = 0
 TALL = 512
+UNROLL = 4
+PANE = 512
 MESH = pl.DeviceIdType.MESH
 f32 = jnp.float32
 bf16 = jnp.bfloat16
@@ -47,8 +49,8 @@
 
 def front_kernel(
     diag_hbm, mask_hbm, panel_hbm, slab_hbm, mine, slab, growth_ref,
-    diag, mask, ah, al, w, wh, wl, rh, rl, gh, gl, need, peak, cols_in, rows_in,
-    diag_sem, mask_sem, panel_sem, slab_sem, self_sem, out_sem, in_sem, line_send, line_recv, ring_send, ring_recv,
+    diag, mask, gram, ah, al, w, wh, wl, rh, rl, gh, gl, need, peak, cols_in, rows_in,
+    diag_sem, mask_sem, panel_sem, slab_sem, out_sem, in_sem, line_send, line_recv, ring_send, ring_recv,
     col_send, col_recv, row_send, row_recv,
 ):
     row, col = lax.axis_index("row"), lax.axis_index("col")
@@ -60,8 +62,8 @@
     rows, cols = lax.axis_size("row"), lax.axis_size("col")
 
     is_source = row < 4
-    is_self = jnp.logical_and(row == 0, y == 0)
-    source = (y, z * 2 + core)
+    source = (y, ((y + 2 + z) % 4) * 2 + core)
+    target_z = (y - row + 18) % 4
 
     def along_x(step):
         return z * 4 + (x + step) % 4
@@ -81,18 +83,12 @@
     def greet(device):
         pl.semaphore_signal(barrier, inc=1, device_id=device, device_id_type=MESH)
 
-    @pl.when(jnp.logical_not(is_self))
-    def _():
-        greet(source)
+    greet(source)
 
     @pl.when(is_source)
     def _():
-        for dx in range(1, 4):
-            greet((y * 4 + dx, row * 2 + core))
-
-    @pl.when(jnp.logical_and(is_source, jnp.logical_not(is_self)))
-    def _():
-        greet((y * 4, row * 2 + core))
+        for step in range(4):
+            greet((target_z * 4 + (row + step) % 4, row * 2 + core))
 
     for step in range(1, 4):
         greet((along_x(step), col))
@@ -100,48 +96,27 @@
     for d in range(1, cols):
         greet((row, (col + d) % cols))
 
-    others = 1 - is_self.astype(jnp.int32)
-    pl.semaphore_wait(barrier, 5 + cols + others + jnp.where(is_source, 3 + others, 0))
+    pl.semaphore_wait(barrier, 6 + cols + jnp.where(is_source, 4, 0))
 
     def spot(which, dz, dx):
         if which == 0:
             return (dz * 4 + dx) * piece
         return half + (dx * 4 + dz) * piece
 
-    def scatter(which, dx):
-        start = spot(which, y, dx)
-        return (
-            panel_hbm.at[rows_at(core * 2 * half + start, piece)],
-            need.at[rows_at(start, piece)],
-            (y * 4 + dx, row * 2 + core),
+    def scatter(which, step):
+        dx = (row + step) % 4
+        start = spot(which, target_z, dx)
+        return pltpu.make_async_remote_copy(
+            src_ref=panel_hbm.at[rows_at(core * 2 * half + start, piece)], dst_ref=need.at[rows_at(start, piece)],
+            send_sem=out_sem.at[which * 4 + step], recv_sem=in_sem.at[which],
+            device_id=(target_z * 4 + dx, row * 2 + core), device_id_type=MESH,
         )
-
-    def remote(which, dx):
-        src, dst, device = scatter(which, dx)
-        return pltpu.make_async_remote_copy(
-            src_ref=src, dst_ref=dst, send_sem=out_sem.at[which * 4 + dx], recv_sem=in_sem.at[which],
-            device_id=device, device_id_type=MESH,
-        )
-
-    def own(which):
-        src, dst, _ = scatter(which, 0)
-        return pltpu.make_async_copy(src, dst, self_sem.at[which])
 
     @pl.when(is_source)
     def _():
         for which in range(2):
-            for dx in range(1, 4):
-                remote(which, dx).start()
-
-    @pl.when(jnp.logical_and(is_source, jnp.logical_not(is_self)))
-    def _():
-        for which in range(2):
-            remote(which, 0).start()
-
-    @pl.when(is_self)
-    def _():
-        for which in range(2):
-            own(which).start()
+            for step in (2, 1, 3, 0):
+                scatter(which, step).start()
 
     fetch_panel.start()
 
@@ -176,7 +151,8 @@
     scale_cols = lax.rsqrt(jnp.sum(on_diag, axis=0, keepdims=True))
     scaled = a * scale_rows * scale_cols
     ah[...], al[...] = split(scaled)
-    w[...] = jnp.where(r_id == c_id, 1.5 - 0.5 * scaled, jnp.where(r_id > c_id, -scaled, 0.0))
+    w[...] = jnp.where(r_id == c_id, 1.0, 0.0)
+    gram[...] = scaled
 
     rb = lax.broadcasted_iota(jnp.int32, (B, B), 0)
     cb = lax.broadcasted_iota(jnp.int32, (B, B), 1)
@@ -191,10 +167,20 @@
         w[B:, B:] += nn(p11, w1[:, B:])
 
     def coarse(_, carry):
+        g00, g10, g11 = gram[:B, :B], gram[B:, :B], gram[B:, B:]
         w0, w1 = w[:B, :B].astype(bf16), w[B:, :].astype(bf16)
-        y0 = nn(w0, ah[:B, :B]).astype(bf16)
-        y1 = nn(w1, ah[...]).astype(bf16)
-        apply(w0, w1, nt(y0, w0), nt(y1[:, :B], w0), nt(y1, w1))
+        p00, p10, p11 = correction(g00), (-g10).astype(bf16), correction(g11)
+        b00, b10, b11 = g00.astype(bf16), g10.astype(bf16), g11.astype(bf16)
+        z00 = g00 + nn(p00, b00)
+        z10 = g10 + (nn(p10, b00) + nn(p11, b10))
+        z11 = g11 + (nt(p10, b10) + nn(p11, b11))
+        c00, c10, c11 = z00.astype(bf16), z10.astype(bf16), z11.astype(bf16)
+        gram[:B, :B] = z00 + nt(c00, p00)
+        gram[B:, :B] = z10 + nt(c10, p00)
+        gram[B:, B:] = z11 + (nt(c10, p10) + nt(c11, p11))
+        w[:B, :B] += nn(p00, w0)
+        w[B:, :B] += nn(p10, w0) + nn(p11, w1[:, :B])
+        w[B:, B:] += nn(p11, w1[:, B:])
         return carry
 
     def fine(_, carry):
@@ -209,15 +195,8 @@
 
     lax.fori_loop(0, COARSE, coarse, 0)
 
-    @pl.when(jnp.logical_not(is_self))
-    def _():
-        for which in range(2):
-            remote(which, 0).wait_recv()
-
-    @pl.when(is_self)
-    def _():
-        for which in range(2):
-            own(which).wait()
+    for which in range(2):
+        scatter(which, 0).wait_recv()
 
     for which in range(2):
         for copy in line_hops(which):
@@ -235,18 +214,27 @@
         second = nt3(lh, ll, wh[B:, :B], wl[B:, :B]) + nt3(qh, ql, wh[B:, B:], wl[B:, B:])
         return first, second
 
-    tiles = mine.shape[0] // B
+    def marked(ref, start, size, first_block):
+        halves = []
+        for k in range(2):
+            parts = [
+                ref[rows_at(start + at, B), k * B:(k + 1) * B] * mask[k, first_block + at // B].astype(f32)
+                for at in range(0, size, B)
+            ]
+            halves.append(jnp.concatenate(parts, axis=0))
+        return halves
+
+    panes = mine.shape[0] // PANE
 
     def solve_mine(t, carry):
-        part = rows_at(t * B, B)
-        block = row * tiles + t
-        parts = solve(mine[part, :B] * mask[0, block].astype(f32), mine[part, B:] * mask[1, block].astype(f32))
+        part = rows_at(t * PANE, PANE)
+        parts = solve(*marked(mine, t * PANE, PANE, (row * panes + t) * (PANE // B)))
         for at, value in zip((0, B), parts):
             mine[part, at:at + B] = value
             rh[part, at:at + B], rl[part, at:at + B] = split(value)
         return carry
 
-    lax.fori_loop(0, EARLY, solve_mine, 0)
+    lax.fori_loop(0, EARLY, solve_mine, 0, unroll=True)
     for which in range(2):
         for copy in line_hops(which):
             copy.wait_recv()
@@ -254,7 +242,7 @@
         for which in range(2):
             for sign in (1, -1):
                 ring_hop(which, sign, stage).start()
-    lax.fori_loop(EARLY, tiles, solve_mine, 0)
+    lax.fori_loop(EARLY, panes, solve_mine, 0, unroll=True)
     for which in range(2):
         for sign in (1, -1):
             ring_hop(which, sign, 0).wait_recv()
@@ -287,7 +275,7 @@
                 peak[0] = jnp.maximum(peak[0], size)
             return carry
 
-        lax.fori_loop(0, mine.shape[0] // TALL, update_rows, 0)
+        lax.fori_loop(0, mine.shape[0] // TALL, update_rows, 0, unroll=UNROLL)
 
     fetch_slab.wait()
     update(0)
@@ -333,14 +321,9 @@
 
     @pl.when(is_source)
     def _():
-        for dx in range(1, 4):
-            for which in range(2):
-                remote(which, dx).wait_send()
-
-    @pl.when(jnp.logical_and(is_source, jnp.logical_not(is_self)))
-    def _():
         for which in range(2):
-            remote(which, 0).wait_send()
+            for step in range(4):
+                scatter(which, step).wait_send()
 
     for d in range(1, cols):
         share_cols(d).wait_send()
@@ -385,6 +368,7 @@
         scratch_shapes=[
             pltpu.VMEM((PW, PW), f32),
             pltpu.SMEM(marks.shape, jnp.int32),
+            pltpu.VMEM((PW, PW), f32),
             pltpu.VMEM((PW, PW), bf16),
             pltpu.VMEM((PW, PW), bf16),
             pltpu.VMEM((PW, PW), f32),
@@ -402,7 +386,6 @@
             dma,
             dma,
             dma,
-            dma((2,)),
             dma((8,)),
             dma((2,)),
             dma((6,)),

time: 59.8 us -> 56.1 us (0.938)
  Pallas kernels: 57.3 us -> 53.6 us
    pallas_call x1, Pallas kernels: 52.7 us -> 49 us  [body(): pl.pallas_call(front_kernel, out_shape=(jax.ShapeDtypeStruct((rows_dev, P...]
where the time goes in v3:
time: 56.1 us; the launch traced here: 56 us
  Pallas kernels  53.6 us (96%)
  between operations  2.4 us (4%)
    pallas_call x1, Pallas kernels, body(): pl.pallas_call(front_kernel, out_shape=(jax.ShapeDtypeStruct((rows_dev, P...  49 us
    pallas_call x1, Pallas kernels, body(): pl.pallas_call(store_kernel, out_shape=(jax.ShapeDtypeStruct((rows_dev, P...  4.63 us

profile of v3, /device:TPU:1, one launch (start us, length us, event | category | flops | bytes accessed | tf_op | source)
XLA Modules:
  0.0 56.0 jit_solution(6522803064009863446)
XLA Ops:
  0.6 49.0 %front.1 = (f32[2048,512]{1,0:T(8,128)S(1)}, f32[2048,1024]{1,0:T(8,128)S(1)}, f32[1,1]{1,0:T(1,128)}) custom-call(f32[512,512]{1,0:T(8,128)} %diag_hbm.1, s32[2,128]{1,0:T(2,128)} %bitcast.2, f32[2048,512]{1,0:T(8,128)} %panel_hbm.1, f32[2048,1024]{1,0:T(8,128)} %slab_hbm.1), custom_call_target="tpu_custom_call" | custom-call | tf_op jit(solution)/shard_map/front/pallas_call | solution.py:359
  49.6 4.6 %store.1 = (f32[2048,512]{1,0:T(8,128)}, f32[2048,1024]{1,0:T(8,128)}) custom-call(f32[2048,512]{1,0:T(8,128)S(1)} %get-tuple-element.8.rows_ref, f32[2048,1024]{1,0:T(8,128)S(1)} %get-tuple-element.9.slab_ref), custom_call_target="tpu_custom_call" | custom-call | tf_op jit(solution)/shard_map/store/pallas_call | solution.py:406

commit v4 on v3

--- a/solution.py
+++ b/solution.py
@@ -13,6 +13,7 @@
 TALL = 512
 UNROLL = 4
 PANE = 512
+PASSED = {1: (0, 1), -1: (3, 2)}
 MESH = pl.DeviceIdType.MESH
 f32 = jnp.float32
 bf16 = jnp.bfloat16
@@ -49,7 +50,7 @@
 
 def front_kernel(
     diag_hbm, mask_hbm, panel_hbm, slab_hbm, mine, slab, growth_ref,
-    diag, mask, gram, ah, al, w, wh, wl, rh, rl, gh, gl, need, peak, cols_in, rows_in,
+    diag, mask, gram, ah, al, w, wh, wl, rh, rl, gh, gl, need, peak, told, cols_in, rows_in,
     diag_sem, mask_sem, panel_sem, slab_sem, out_sem, in_sem, line_send, line_recv, ring_send, ring_recv,
     col_send, col_recv, row_send, row_recv,
 ):
@@ -135,12 +136,18 @@
             hop(line, 3 * which + step - 1, spot(which, z, x), piece, along(step)) for step in (2, 1, 3)
         ]
 
-    def ring_hop(which, sign, stage):
-        at, along = ((z, along_z), (x, along_x))[which]
-        owner = at if stage < 2 else (at + 4 - sign) % 4
-        part = stage % 2 if sign == 1 else 1 - stage % 2
-        index = which * 6 + (0 if sign == 1 else 3) + stage
-        return hop(ring, index, half * which + owner * wide + part * (wide // 2), wide // 2, along(sign % 4))
+    def ring_hop(which, sign, index):
+        at, fine_at, along = ((z, x, along_z), (x, z, along_x))[which]
+        owner, offset = (at, index) if index < 4 else ((at + 4 - sign) % 4, PASSED[sign][index - 4])
+        start = half * which + owner * wide + ((fine_at + offset) % 4) * piece
+        return hop(ring, which * 12 + (0 if sign == 1 else 6) + index, start, piece, along(sign % 4))
+
+    def ring_hops(plus, minus):
+        for k in range(max(len(plus), len(minus))):
+            for which in range(2):
+                for sign, indices in ((1, plus), (-1, minus)):
+                    if k < len(indices):
+                        yield ring_hop(which, sign, indices[k])
 
     fetch_diag.wait()
     a = diag[...]
@@ -201,6 +208,8 @@
     for which in range(2):
         for copy in line_hops(which):
             copy.start()
+    for copy in ring_hops((0,), (0,)):
+        copy.start()
     fetch_slab.start()
     lax.fori_loop(0, FINE, fine, 0)
     wh[...], wl[...] = split(w[...] * scale_cols)
@@ -238,15 +247,13 @@
     for which in range(2):
         for copy in line_hops(which):
             copy.wait_recv()
-    for stage in range(2):
-        for which in range(2):
-            for sign in (1, -1):
-                ring_hop(which, sign, stage).start()
+    for copy in ring_hops((1, 2, 3), (3, 2, 1)):
+        copy.start()
+    for copy in ring_hops((0,), (0,)):
+        copy.wait_recv()
+    for copy in ring_hops((4,), ()):
+        copy.start()
     lax.fori_loop(EARLY, panes, solve_mine, 0, unroll=True)
-    for which in range(2):
-        for sign in (1, -1):
-            ring_hop(which, sign, 0).wait_recv()
-            ring_hop(which, sign, 2).start()
 
     def masked_need(which, step):
         start = half * which + (((z, x)[which] + step) % 4) * wide
@@ -272,21 +279,23 @@
                 value = slab[part, at] - value
                 slab[part, at] = value
                 size = jnp.max(jnp.abs(value).reshape(-1, 8, wide), axis=0)
-                peak[0] = jnp.maximum(peak[0], size)
+                peak[...] = jnp.maximum(peak[...], size)
             return carry
 
         lax.fori_loop(0, mine.shape[0] // TALL, update_rows, 0, unroll=UNROLL)
 
     fetch_slab.wait()
     update(0)
-    for which in range(2):
-        for sign in (1, -1):
-            ring_hop(which, sign, 1).wait_recv()
+    for copy in ring_hops((1,), (3, 2)):
+        copy.wait_recv()
+    for copy in ring_hops((5,), (4, 5)):
+        copy.start()
+    for copy in ring_hops((2, 3), (1,)):
+        copy.wait_recv()
     update(1)
     update(3)
-    for which in range(2):
-        for sign in (1, -1):
-            ring_hop(which, sign, 2).wait_recv()
+    for copy in ring_hops((4, 5), (4, 5)):
+        copy.wait_recv()
     update(2)
 
     def share(src, dst, sems, d, device):
@@ -296,28 +305,28 @@
         )
 
     def share_cols(d):
-        return share(peak.at[0], cols_in, (col_send, col_recv), d, (row, (col + d) % cols))
+        return share(told.at[0], cols_in, (col_send, col_recv), d, (row, (col + d) % cols))
 
     def share_rows(d):
-        return share(peak.at[1], rows_in, (row_send, row_recv), d, ((row + d) % rows, col))
-
+        return share(told.at[1], rows_in, (row_send, row_recv), d, ((row + d) % rows, col))
+
+    best = jnp.max(peak[...], axis=0, keepdims=True)
+    told[0] = best
     for d in far_first(cols):
         share_cols(d).start()
-    best = peak[0]
     for d in range(1, cols):
         share_cols(d).wait_recv()
     for d in range(1, cols):
         best = jnp.maximum(best, cols_in[d - 1])
-    peak[1] = best
+    told[1] = best
     for d in far_first(rows):
         share_rows(d).start()
 
     for which in range(2):
         for copy in line_hops(which):
             copy.wait_send()
-        for sign in (1, -1):
-            for stage in range(3):
-                ring_hop(which, sign, stage).wait_send()
+    for copy in ring_hops(range(6), range(6)):
+        copy.wait_send()
 
     @pl.when(is_source)
     def _():
@@ -379,9 +388,10 @@
             pltpu.VMEM((B, PW), bf16),
             pltpu.VMEM((B, PW), bf16),
             pltpu.VMEM((cols_dev, PW), f32),
-            pltpu.VMEM((2, 8, 128), f32),
-            pltpu.VMEM((n_cols - 1, 8, 128), f32),
-            pltpu.VMEM((n_rows - 1, 8, 128), f32),
+            pltpu.VMEM((8, 128), f32),
+            pltpu.VMEM((2, 1, 128), f32),
+            pltpu.VMEM((n_cols - 1, 1, 128), f32),
+            pltpu.VMEM((n_rows - 1, 1, 128), f32),
             dma,
             dma,
             dma,
@@ -390,8 +400,8 @@
             dma((2,)),
             dma((6,)),
             dma((6,)),
-            dma((12,)),
-            dma((12,)),
+            dma((24,)),
+            dma((24,)),
             dma((n_cols - 1,)),
             dma((n_cols - 1,)),
             dma((n_rows - 1,)),

time: 56.1 us -> 55 us (0.980)
  Pallas kernels: 53.6 us -> 52.3 us
    pallas_call x1, Pallas kernels: 49 us -> 47.7 us  [body(): pl.pallas_call(front_kernel, out_shape=(jax.ShapeDtypeStruct((rows_dev, P...]
where the time goes in v4:
time: 55 us; the launch traced here: 54.7 us
  Pallas kernels  52.3 us (95%)
  between operations  2.4 us (4%)
    pallas_call x1, Pallas kernels, body(): pl.pallas_call(front_kernel, out_shape=(jax.ShapeDtypeStruct((rows_dev, P...  47.7 us
    pallas_call x1, Pallas kernels, body(): pl.pallas_call(store_kernel, out_shape=(jax.ShapeDtypeStruct((rows_dev, P...  4.63 us

profile of v4, /device:TPU:1, one launch (start us, length us, event | category | flops | bytes accessed | tf_op | source)
XLA Modules:
  0.0 54.7 jit_solution(3062094958805738007)
XLA Ops:
  0.6 47.7 %front.1 = (f32[2048,512]{1,0:T(8,128)S(1)}, f32[2048,1024]{1,0:T(8,128)S(1)}, f32[1,1]{1,0:T(1,128)}) custom-call(f32[512,512]{1,0:T(8,128)} %diag_hbm.1, s32[2,128]{1,0:T(2,128)} %bitcast.2, f32[2048,512]{1,0:T(8,128)} %panel_hbm.1, f32[2048,1024]{1,0:T(8,128)} %slab_hbm.1), custom_call_target="tpu_custom_call" | custom-call | tf_op jit(solution)/shard_map/front/pallas_call | solution.py:368
  48.3 4.6 %store.1 = (f32[2048,512]{1,0:T(8,128)}, f32[2048,1024]{1,0:T(8,128)}) custom-call(f32[2048,512]{1,0:T(8,128)S(1)} %get-tuple-element.8.rows_ref, f32[2048,1024]{1,0:T(8,128)S(1)} %get-tuple-element.9.slab_ref), custom_call_target="tpu_custom_call" | custom-call | tf_op jit(solution)/shard_map/store/pallas_call | solution.py:416

commit v5 on v4

--- a/solution.py
+++ b/solution.py
@@ -9,8 +9,8 @@
 PW = 512
 COARSE = 7
 FINE = 2
-EARLY = 0
 TALL = 512
+CHUNK = 512
 UNROLL = 4
 PANE = 512
 PASSED = {1: (0, 1), -1: (3, 2)}
@@ -132,9 +132,7 @@
 
     def line_hops(which):
         along = (along_x, along_z)[which]
-        return [
-            hop(line, 3 * which + step - 1, spot(which, z, x), piece, along(step)) for step in (2, 1, 3)
-        ]
+        return {step: hop(line, 3 * which + step - 1, spot(which, z, x), piece, along(step)) for step in (2, 1, 3)}
 
     def ring_hop(which, sign, index):
         at, fine_at, along = ((z, x, along_z), (x, z, along_x))[which]
@@ -142,12 +140,11 @@
         start = half * which + owner * wide + ((fine_at + offset) % 4) * piece
         return hop(ring, which * 12 + (0 if sign == 1 else 6) + index, start, piece, along(sign % 4))
 
-    def ring_hops(plus, minus):
+    def ring_hops(which, plus, minus):
         for k in range(max(len(plus), len(minus))):
-            for which in range(2):
-                for sign, indices in ((1, plus), (-1, minus)):
-                    if k < len(indices):
-                        yield ring_hop(which, sign, indices[k])
+            for sign, indices in ((1, plus), (-1, minus)):
+                if k < len(indices):
+                    yield ring_hop(which, sign, indices[k])
 
     fetch_diag.wait()
     a = diag[...]
@@ -201,18 +198,38 @@
         return carry
 
     lax.fori_loop(0, COARSE, coarse, 0)
-
-    for which in range(2):
-        scatter(which, 0).wait_recv()
-
-    for which in range(2):
-        for copy in line_hops(which):
-            copy.start()
-    for copy in ring_hops((0,), (0,)):
-        copy.start()
-    fetch_slab.start()
     lax.fori_loop(0, FINE, fine, 0)
     wh[...], wl[...] = split(w[...] * scale_cols)
+
+    def begin(which):
+        scatter(which, 0).wait_recv()
+        for copy in line_hops(which).values():
+            copy.start()
+        for copy in ring_hops(which, (0,), (0,)):
+            copy.start()
+
+    def feed_near(which):
+        for step in (1, 3):
+            line_hops(which)[step].wait_recv()
+        for copy in ring_hops(which, (1, 3), (3, 1)):
+            copy.start()
+
+    def feed_far(which):
+        line_hops(which)[2].wait_recv()
+        for copy in ring_hops(which, (2,), (2,)):
+            copy.start()
+
+    def pass_on(which):
+        for copy in ring_hops(which, (0, 1), (0, 3, 2)):
+            copy.wait_recv()
+        for copy in ring_hops(which, (4, 5), (4, 5)):
+            copy.start()
+        for copy in ring_hops(which, (3, 2), (1,)):
+            copy.wait_recv()
+
+    begin(0)
+    begin(1)
+    fetch_slab.start()
     fetch_panel.wait()
     fetch_mask.wait()
 
@@ -243,17 +260,13 @@
             rh[part, at:at + B], rl[part, at:at + B] = split(value)
         return carry
 
-    lax.fori_loop(0, EARLY, solve_mine, 0, unroll=True)
-    for which in range(2):
-        for copy in line_hops(which):
-            copy.wait_recv()
-    for copy in ring_hops((1, 2, 3), (3, 2, 1)):
-        copy.start()
-    for copy in ring_hops((0,), (0,)):
-        copy.wait_recv()
-    for copy in ring_hops((4,), ()):
-        copy.start()
-    lax.fori_loop(EARLY, panes, solve_mine, 0, unroll=True)
+    lax.fori_loop(0, panes // 2, solve_mine, 0, unroll=True)
+    feed_near(0)
+    feed_far(0)
+    lax.fori_loop(panes // 2, 3 * panes // 4, solve_mine, 0, unroll=True)
+    feed_near(1)
+    lax.fori_loop(3 * panes // 4, panes, solve_mine, 0, unroll=True)
+    feed_far(1)
 
     def masked_need(which, step):
         start = half * which + (((z, x)[which] + step) % 4) * wide
@@ -265,9 +278,9 @@
 
     peak[...] = jnp.zeros_like(peak)
 
-    def update(step):
-        at0, left0, right0 = masked_need(0, step)
-        at1, left1, right1 = masked_need(1, step)
+    def update(one, two):
+        at0, left0, right0 = masked_need(*one)
+        at1, left1, right1 = masked_need(*two)
         first, second = solve(jnp.concatenate([left0, left1], axis=0), jnp.concatenate([right0, right1], axis=0))
         gh[:, :B], gl[:, :B] = split(first)
         gh[:, B:], gl[:, B:] = split(second)
@@ -285,18 +298,15 @@
         lax.fori_loop(0, mine.shape[0] // TALL, update_rows, 0, unroll=UNROLL)
 
     fetch_slab.wait()
-    update(0)
-    for copy in ring_hops((1,), (3, 2)):
-        copy.wait_recv()
-    for copy in ring_hops((5,), (4, 5)):
-        copy.start()
-    for copy in ring_hops((2, 3), (1,)):
-        copy.wait_recv()
-    update(1)
-    update(3)
-    for copy in ring_hops((4, 5), (4, 5)):
-        copy.wait_recv()
-    update(2)
+    update((0, 0), (1, 0))
+    pass_on(0)
+    update((0, 1), (0, 3))
+    pass_on(1)
+    update((1, 1), (1, 3))
+    for which in range(2):
+        for copy in ring_hops(which, (4, 5), (4, 5)):
+            copy.wait_recv()
+    update((0, 2), (1, 2))
 
     def share(src, dst, sems, d, device):
         return pltpu.make_async_remote_copy(
@@ -323,10 +333,10 @@
         share_rows(d).start()
 
     for which in range(2):
-        for copy in line_hops(which):
+        for copy in line_hops(which).values():
             copy.wait_send()
-    for copy in ring_hops(range(6), range(6)):
-        copy.wait_send()
+        for copy in ring_hops(which, range(6), range(6)):
+            copy.wait_send()
 
     @pl.when(is_source)
     def _():
@@ -348,8 +358,8 @@
 def store_kernel(rows_ref, slab_ref, rows_out, slab_out, sems):
     copies = []
     for src, dst in ((slab_ref, slab_out), (rows_ref, rows_out)):
-        for at in range(0, src.shape[0], TALL):
-            part = pl.ds(at, TALL)
+        for at in range(0, src.shape[0], CHUNK):
+            part = pl.ds(at, CHUNK)
             copies.append(pltpu.make_async_copy(src.at[part], dst.at[part], sems.at[len(copies)]))
     for copy in copies:
         copy.start()
@@ -421,7 +431,7 @@
         ),
         in_specs=[vmem, vmem],
         out_specs=(hbm, hbm),
-        scratch_shapes=[dma((2 * rows_dev // TALL,))],
+        scratch_shapes=[dma((2 * rows_dev // CHUNK,))],
         compiler_params=pltpu.CompilerParams(vmem_limit_bytes=1 << 20),
         name="store",
     )(rows, updated)

time: 55 us -> 53.8 us (0.978)
  Pallas kernels: 52.3 us -> 51.1 us
    pallas_call x1, Pallas kernels: 47.7 us -> 46.5 us  [body(): pl.pallas_call(front_kernel, out_shape=(jax.ShapeDtypeStruct((rows_dev, P...]
where the time goes in v5:
time: 53.8 us; the launch traced here: 53.5 us
  Pallas kernels  51.1 us (95%)
  between operations  2.4 us (4%)
    pallas_call x1, Pallas kernels, body(): pl.pallas_call(front_kernel, out_shape=(jax.ShapeDtypeStruct((rows_dev, P...  46.5 us
    pallas_call x1, Pallas kernels, body(): pl.pallas_call(store_kernel, out_shape=(jax.ShapeDtypeStruct((rows_dev, P...  4.63 us

profile of v5, /device:TPU:1, one launch (start us, length us, event | category | flops | bytes accessed | tf_op | source)
XLA Modules:
  0.0 53.5 jit_solution(5631876325820367607)
XLA Ops:
  0.6 46.5 %front.1 = (f32[2048,512]{1,0:T(8,128)S(1)}, f32[2048,1024]{1,0:T(8,128)S(1)}, f32[1,1]{1,0:T(1,128)}) custom-call(f32[512,512]{1,0:T(8,128)} %diag_hbm.1, s32[2,128]{1,0:T(2,128)} %bitcast.2, f32[2048,512]{1,0:T(8,128)} %panel_hbm.1, f32[2048,1024]{1,0:T(8,128)} %slab_hbm.1), custom_call_target="tpu_custom_call" | custom-call | tf_op jit(solution)/shard_map/front/pallas_call | solution.py:378
  47.1 4.6 %store.1 = (f32[2048,512]{1,0:T(8,128)}, f32[2048,1024]{1,0:T(8,128)}) custom-call(f32[2048,512]{1,0:T(8,128)S(1)} %get-tuple-element.8.rows_ref, f32[2048,1024]{1,0:T(8,128)S(1)} %get-tuple-element.9.slab_ref), custom_call_target="tpu_custom_call" | custom-call | tf_op jit(solution)/shard_map/store/pallas_call | solution.py:426

commit v6 on v5

--- a/solution.py
+++ b/solution.py
@@ -7,7 +7,7 @@
 
 B = 256
 PW = 512
-COARSE = 7
+COARSE = 8
 FINE = 2
 TALL = 512
 CHUNK = 512

time: 53.8 us -> 54.5 us (1.013)
  Pallas kernels: 51.1 us -> 51.8 us
    pallas_call x1, Pallas kernels: 46.5 us -> 47.2 us  [body(): pl.pallas_call(front_kernel, out_shape=(jax.ShapeDtypeStruct((rows_dev, P...]
where the time goes in v6:
time: 54.5 us; the launch traced here: 54.2 us
  Pallas kernels  51.8 us (95%)
  between operations  2.4 us (4%)
    pallas_call x1, Pallas kernels, body(): pl.pallas_call(front_kernel, out_shape=(jax.ShapeDtypeStruct((rows_dev, P...  47.2 us
    pallas_call x1, Pallas kernels, body(): pl.pallas_call(store_kernel, out_shape=(jax.ShapeDtypeStruct((rows_dev, P...  4.63 us

profile of v6, /device:TPU:1, one launch (start us, length us, event | category | flops | bytes accessed | tf_op | source)
XLA Modules:
  0.0 54.2 jit_solution(10804010000674704995)
XLA Ops:
  0.6 47.2 %front.1 = (f32[2048,512]{1,0:T(8,128)S(1)}, f32[2048,1024]{1,0:T(8,128)S(1)}, f32[1,1]{1,0:T(1,128)}) custom-call(f32[512,512]{1,0:T(8,128)} %diag_hbm.1, s32[2,128]{1,0:T(2,128)} %bitcast.2, f32[2048,512]{1,0:T(8,128)} %panel_hbm.1, f32[2048,1024]{1,0:T(8,128)} %slab_hbm.1), custom_call_target="tpu_custom_call" | custom-call | tf_op jit(solution)/shard_map/front/pallas_call | solution.py:378
  47.8 4.6 %store.1 = (f32[2048,512]{1,0:T(8,128)}, f32[2048,1024]{1,0:T(8,128)}) custom-call(f32[2048,512]{1,0:T(8,128)S(1)} %get-tuple-element.8.rows_ref, f32[2048,1024]{1,0:T(8,128)S(1)} %get-tuple-element.9.slab_ref), custom_call_target="tpu_custom_call" | custom-call | tf_op jit(solution)/shard_map/store/pallas_call | solution.py:426

commit v7 on v5

--- a/solution.py
+++ b/solution.py
@@ -97,7 +97,9 @@
     for d in range(1, cols):
         greet((row, (col + d) % cols))
 
-    pl.semaphore_wait(barrier, 6 + cols + jnp.where(is_source, 4, 0))
+    @pl.when(is_source)
+    def _():
+        pl.semaphore_wait(barrier, 10 + cols)
 
     def spot(which, dz, dx):
         if which == 0:
@@ -200,6 +202,10 @@
     lax.fori_loop(0, COARSE, coarse, 0)
     lax.fori_loop(0, FINE, fine, 0)
     wh[...], wl[...] = split(w[...] * scale_cols)
+
+    @pl.when(jnp.logical_not(is_source))
+    def _():
+        pl.semaphore_wait(barrier, 6 + cols)
 
     def begin(which):
         scatter(which, 0).wait_recv()

time: 53.8 us -> 54.4 us (1.011)
  Pallas kernels: 51.1 us -> 51.7 us
    pallas_call x1, Pallas kernels: 46.5 us -> 47 us  [body(): pl.pallas_call(front_kernel, out_shape=(jax.ShapeDtypeStruct((rows_dev, P...]
where the time goes in v7:
time: 54.4 us; the launch traced here: 54.1 us
  Pallas kernels  51.7 us (95%)
  between operations  2.4 us (4%)
    pallas_call x1, Pallas kernels, body(): pl.pallas_call(front_kernel, out_shape=(jax.ShapeDtypeStruct((rows_dev, P...  47 us
    pallas_call x1, Pallas kernels, body(): pl.pallas_call(store_kernel, out_shape=(jax.ShapeDtypeStruct((rows_dev, P...  4.63 us

profile of v7, /device:TPU:1, one launch (start us, length us, event | category | flops | bytes accessed | tf_op | source)
XLA Modules:
  0.0 54.1 jit_solution(6601901101247023799)
XLA Ops:
  0.6 47.0 %front.1 = (f32[2048,512]{1,0:T(8,128)S(1)}, f32[2048,1024]{1,0:T(8,128)S(1)}, f32[1,1]{1,0:T(1,128)}) custom-call(f32[512,512]{1,0:T(8,128)} %diag_hbm.1, s32[2,128]{1,0:T(2,128)} %bitcast.2, f32[2048,512]{1,0:T(8,128)} %panel_hbm.1, f32[2048,1024]{1,0:T(8,128)} %slab_hbm.1), custom_call_target="tpu_custom_call" | custom-call | tf_op jit(solution)/shard_map/front/pallas_call | solution.py:384
  47.7 4.6 %store.1 = (f32[2048,512]{1,0:T(8,128)}, f32[2048,1024]{1,0:T(8,128)}) custom-call(f32[2048,512]{1,0:T(8,128)S(1)} %get-tuple-element.8.rows_ref, f32[2048,1024]{1,0:T(8,128)S(1)} %get-tuple-element.9.slab_ref), custom_call_target="tpu_custom_call" | custom-call | tf_op jit(solution)/shard_map/store/pallas_call | solution.py:432
